TPU v7x, 256 devices: a whole 4x4x8 slice. The times are simulated.
256 devices in a mesh: row: 64 (over x, y_lo, z), panel: 4 (over y_hi, core).
Axes of the slice: x: 4, y: 4 (y_hi: 2, y_lo: 2; y = y_hi * 2 + y_lo), z: 8, core: 2. Of those that a mesh axis runs over, the one named last changes fastest.
Arguments:
- pixel_ids: int32 [65536], P('row'), may hold values from 0 to 65535, each once
- quad_offsets: int32 [2, 16, 65536], P(None, None, 'row'), may hold values from 0 to 7
- prior_factor: float32 [65536, 2048], P('row', 'panel'), may hold values from -0.036 to 0.036, as said below
Outputs:
- panel_factor: float32 [65536, 1024], P(('row', 'panel'))
Inputs may be any that keep to these rules, and one draw needn't show every extreme that they name: `pixel_ids`: each pixel of the grid appears in exactly one row. `prior_factor`: schur[panel_index] is positive definite.
All inputs are finite; a program needn't handle non-finite values.
Results may differ from a plain program's by a relative error of at most 0.0003.
Values sent between devices are 32-bit elements; how exact they have to be, the bound alone decides.
A program may use at most 128 MiB of HBM per device.

v0:
```python
import jax
import jax.numpy as jnp
from jax import lax
from jax.sharding import PartitionSpec as P

B = 1024
range_inverse = 1.0


def from_behind(block, axis, distance):
    devices = range(lax.axis_size(axis))
    route = [((i - distance) % len(devices), i) for i in devices]
    return lax.ppermute(block, axis, route)


def locate(pixel_ids, quad_offsets):
    column = (pixel_ids % 256).astype(jnp.float32)
    lines = (pixel_ids // 256).astype(jnp.float32)
    east = column[None, :] + (quad_offsets[0].astype(jnp.float32) + 0.5) / 8.0
    north = lines[None, :] + (quad_offsets[1].astype(jnp.float32) + 0.5) / 8.0
    return (east, north)


def cover_tile(east_rows, north_rows, east_cols, north_cols):
    count = east_rows.shape[0]

    def accumulate(index, running):
        east_one = lax.dynamic_index_in_dim(east_rows, index, 0, keepdims=False)
        north_one = lax.dynamic_index_in_dim(north_rows, index, 0, keepdims=False)
        apart_east = east_cols[:, :, None] - east_one[None, None, :]
        apart_north = north_cols[:, :, None] - north_one[None, None, :]
        return running + jnp.sum(
            jnp.exp(-(apart_east * apart_east + apart_north * apart_north) * range_inverse), axis=0
        )

    start = jnp.zeros((east_cols.shape[1], east_rows.shape[1]), jnp.float32)
    total = lax.fori_loop(0, count, accumulate, start)
    return total.T / float(count * count)


def local(pixel_ids, quad_offsets, prior_factor):
    panel_count = lax.axis_size("panel")
    row_count = lax.axis_size("row")
    block_rows = pixel_ids.shape[0]
    quarter_rows = block_rows // panel_count
    per_device = B // (row_count * panel_count)
    span_cols = panel_count * per_device
    row_pos = lax.axis_index("row")
    panel_pos = lax.axis_index("panel")
    east, north = locate(pixel_ids, quad_offsets)
    all_points = jnp.stack([east, north])
    own_points = lax.dynamic_slice_in_dim(all_points, panel_pos * quarter_rows, quarter_rows, 2)
    own_east = own_points[0]
    own_north = own_points[1]
    local_points = all_points.reshape(2, east.shape[0], panel_count, quarter_rows)[
        :, :, :, :per_device
    ]
    local_points = local_points.reshape(2, east.shape[0], span_cols)
    start_cols = jnp.zeros((quarter_rows, B), jnp.float32)

    def place(columns, held, source):
        tile = cover_tile(own_east, own_north, held[0], held[1])
        return lax.dynamic_update_slice(columns, tile, (jnp.int32(0), source * span_cols))

    def turn(index, carry):
        held, columns = carry
        columns = place(columns, held, (row_pos - index) % row_count)
        held = from_behind(held, "row", 1)
        return (held, columns)

    held, columns = lax.fori_loop(0, row_count - 1, turn, (local_points, start_cols))
    columns = place(columns, held, (row_pos - (row_count - 1)) % row_count)
    device_pos = row_pos * panel_count + panel_pos
    row_ids = jnp.arange(quarter_rows, dtype=jnp.int32)[:, None]
    col_ids = jnp.arange(B, dtype=jnp.int32)[None, :]
    on_diagonal = (row_ids < per_device) & (col_ids == device_pos * per_device + row_ids)
    cover = columns + jnp.where(on_diagonal, 1.0, 0.0).astype(jnp.float32)
    whole_rows = lax.all_to_all(prior_factor, "panel", split_axis=0, concat_axis=1, tiled=True)
    panel_prior = lax.all_gather(whole_rows[:per_device], ("row", "panel"), axis=0, tiled=True)
    update = jnp.dot(
        whole_rows,
        panel_prior.T,
        precision=lax.Precision.HIGHEST,
        preferred_element_type=jnp.float32,
    )
    schur = cover - update
    diag_rows = lax.all_gather(schur[:per_device], ("row", "panel"), axis=0, tiled=True)
    diag_factor = jnp.linalg.cholesky(diag_rows)
    return lax.linalg.triangular_solve(
        diag_factor, schur, left_side=False, lower=True, transpose_a=True
    )


def solution(mesh):
    return jax.shard_map(
        local,
        mesh=mesh,
        in_specs=(P("row"), P(None, None, "row"), P("row", "panel")),
        out_specs=P(("row", "panel"), None),
        check_vma=False,
    )
```

profile of v0, /device:TPU:32, one launch (start us, length us, event | category | flops | bytes accessed | tf_op | source)
XLA Modules:
  0.0 1338.7 jit_solution(4955843680710674743)
XLA Ops:
  11.4 26.9 %all-to-all-done = f32[4,256,512]{2,1,0:T(8,128)S(1)} async-done(((f32[4,256,512]{2,1,0:T(8,128)}), f32[4,256,512]{2,1,0:T(8,128)S(1)}, u32[]{:S(2)}, u32[]{:S(2)}) %all-to-all-start) | async-done | bytes 2097184 | tf_op jit(solution)/shard_map/all_to_all | solution.py:78
  39.1 497.6 %while.68 = (s32[]{:T(128)}, f32[2,16,16]{2,1,0:T(8,128)S(1)}, f32[256,1024]{0,1:T(8,128)S(1)}, f32[16,256]{1,0:T(8,128)S(1)}, f32[16,256]{1,0:T(8,128)S(1)}, /*...) while((s32[]{:T(128)}, f32[2,16,16]{2,1,0:T(8,128)S(1)}, ...), condition=%wide.region_4.5_spmd, body=%wide.region_0.4_spmd.sunk | while | flops 466965 | bytes 123403 | solution.py:71
  62.2 4.6 collective-permute-done
  70.2 4.7 collective-permute-done
  78.2 4.7 collective-permute-done
  86.2 4.8 collective-permute-done
  102.2 4.6 collective-permute-done
  110.1 4.6 collective-permute-done
  118.1 4.6 collective-permute-done
  126.0 4.6 collective-permute-done
  134.0 4.7 collective-permute-done
  150.0 4.6 collective-permute-done
  165.8 4.6 collective-permute-done
  181.8 4.6 collective-permute-done
  189.7 4.7 collective-permute-done
  197.7 4.7 collective-permute-done
  213.6 4.6 collective-permute-done
  221.6 4.7 collective-permute-done
  237.5 4.7 collective-permute-done
  253.5 4.7 collective-permute-done
  269.3 4.6 collective-permute-done
  277.3 4.7 collective-permute-done
  309.1 4.7 collective-permute-done
  333.0 4.7 collective-permute-done
  349.0 4.7 collective-permute-done
  364.9 4.6 collective-permute-done
  372.8 4.6 collective-permute-done
  380.8 4.6 collective-permute-done
  388.8 4.6 collective-permute-done
  396.7 4.7 collective-permute-done
  412.6 4.6 collective-permute-done
  420.6 4.6 collective-permute-done
  428.6 4.6 collective-permute-done
  436.5 4.6 collective-permute-done
  444.5 4.6 collective-permute-done
  452.4 4.6 collective-permute-done
  468.4 4.6 collective-permute-done
  476.3 4.6 collective-permute-done
  492.3 4.6 collective-permute-done
  500.2 4.6 collective-permute-done
  516.1 4.6 collective-permute-done
  545.9 10.2 reshape.138
  556.0 16.1 %convolution_subtract_fusion = f32[256,1024]{1,0:T(8,128)S(1)} fusion(f32[256,2048]{0,1:T(8,128)S(1)} %bitcast.152, f32[1024,2048]{1,0:T(8,128)} %reshape.138, f32[256,1024]{1,0:T(8,128)S(1)} %dynamic_update_slice.13, s32[256]{0:T(256)S(1)} %iota_add_fusion, pred[256]{0:T(512)(128)(4,1)S(1)} %iota_compare_fusion.4), kind=kOutput, calls=%fused_computation.15 | convolution fusion | flops 6443761664 | bytes 12584192 | tf_op jit(solution)/shard_map/dot_general | solution.py:80
  573.7 412.5 %all-gather.7.cloned.1.call-done = f32[256,4,1024]{2,1,0:T(4,128)} async-done(((f32[1,4,1024]{2,1,0:T(4,128)}), f32[256,4,1024]{2,1,0:T(4,128)}) %all-gather.7.cloned.1.call-update) | async-done | bytes 4194320 | tf_op jit(solution)/shard_map/all_gather | solution.py:87
  986.2 5.3 reshape.140
  991.5 5.8 copy.69
  1003.6 11.7 cholesky.223
  1017.9 9.8 custom-call.62
  1031.6 11.9 cholesky.244
  1044.2 9.8 custom-call.63
  1057.3 11.7 cholesky.468
  1069.7 9.8 custom-call.64
  1083.0 11.9 cholesky.487
  1095.5 9.8 custom-call.65
  1108.8 11.7 cholesky.506
  1121.2 10.2 custom-call.66
  1134.7 11.7 cholesky.526
  1147.0 9.8 custom-call.67
  1159.8 11.7 cholesky.546
  1172.2 9.8 custom-call.68
  1184.6 11.7 cholesky.564
  1207.3 4.9 select_select_fusion
  1212.2 22.8 %while.69 = (s32[]{:T(128)}, f32[1024,1024]{1,0:T(8,128)}, s32[8,2]{0,1:T(2,128)S(1)}, f32[8,128,128]{2,1,0:T(8,128)S(1)}, s32[]{:T(128)}) while((s32[]{:T(128)}, f32[1024,1024]{1,0:T(8,128)}, s32[8,2]{0,1:T(2,128)S(1)}, f32[8,128,128]{2,1,0:T(8,128)S(1)}, s32[]{:T(128)}) %tuple.176), condition=%wide.while_cond, body=%wide.while_body.sunk | while | flops 2 | bytes 131189 | solution.py:89
  1235.1 78.8 %custom-call.69 = f32[8,128,128]{1,2,0:T(8,128)S(1)} custom-call(f32[8,128,128]{2,1,0:T(8,128)S(1)} %get-tuple-element.405), custom_call_target="InvertDiagBlocksLowerTriangular" | custom-call | tf_op jit(solution)/shard_map/triangular_solve | solution.py:89
  (3597 shorter events, 577.0 us)
Async XLA Ops:
  6.5 31.8 %all-to-all-start = ((f32[4,256,512]{2,1,0:T(8,128)}), f32[4,256,512]{2,1,0:T(8,128)S(1)}, u32[]{:S(2)}, u32[]{:S(2)}) async-start(f32[4,256,512]{2,1,0:T(8,128)} %bitcast.153), calls=%async_computation | async-start | bytes 4194304 | tf_op jit(solution)/shard_map/all_to_all | solution.py:78
  11.1 534.7 %all-gather.5.cloned.1.call-start = ((), (), s32[]{:S(2)}) async-start(), calls=%async_computation.1 | async-start | bytes 8421376 | tf_op jit(solution)/shard_map/all_gather | solution.py:79
  39.0 947.2 %all-gather.7.cloned.1.call-start = ((), (), s32[]{:S(2)}) async-start(), calls=%async_computation.2 | async-start | bytes 4210688 | tf_op jit(solution)/shard_map/all_gather | solution.py:87
  50.9 8.0 collective-permute-start
  58.9 8.0 collective-permute-start
  66.8 8.0 collective-permute-start
  74.9 8.0 collective-permute-start
  82.9 8.1 collective-permute-start
  90.9 7.9 collective-permute-start
  98.8 8.0 collective-permute-start
  106.8 8.0 collective-permute-start
  114.8 8.0 collective-permute-start
  122.7 8.0 collective-permute-start
  130.7 8.0 collective-permute-start
  138.7 8.0 collective-permute-start
  146.7 8.0 collective-permute-start
  154.6 7.9 collective-permute-start
  162.5 8.0 collective-permute-start
  170.5 8.0 collective-permute-start
  178.5 8.0 collective-permute-start
  186.4 8.0 collective-permute-start
  194.4 8.0 collective-permute-start
  202.4 7.9 collective-permute-start
  210.3 8.0 collective-permute-start
  218.3 8.0 collective-permute-start
  226.3 7.9 collective-permute-start
  234.2 8.0 collective-permute-start
  242.2 7.9 collective-permute-start
  250.1 8.0 collective-permute-start
  258.1 7.9 collective-permute-start
  266.0 8.0 collective-permute-start
  274.0 8.0 collective-permute-start
  282.0 7.9 collective-permute-start
  290.0 7.9 collective-permute-start
  297.9 7.9 collective-permute-start
  305.8 8.0 collective-permute-start
  313.8 8.0 collective-permute-start
  321.8 7.9 collective-permute-start
  329.7 8.0 collective-permute-start
  337.7 7.9 collective-permute-start
  345.6 8.0 collective-permute-start
  353.6 8.0 collective-permute-start
  361.6 8.0 collective-permute-start
  369.5 8.0 collective-permute-start
  377.5 8.0 collective-permute-start
  385.4 8.0 collective-permute-start
  393.4 8.0 collective-permute-start
  401.4 7.9 collective-permute-start
  409.3 8.0 collective-permute-start
  417.3 8.0 collective-permute-start
  425.2 8.0 collective-permute-start
  433.2 8.0 collective-permute-start
  441.2 8.0 collective-permute-start
  449.1 8.0 collective-permute-start
  457.1 8.0 collective-permute-start
  465.1 8.0 collective-permute-start
  473.0 8.0 collective-permute-start
  481.0 8.0 collective-permute-start
  488.9 8.0 collective-permute-start
  496.9 8.0 collective-permute-start
  504.9 8.0 collective-permute-start
  512.8 8.0 collective-permute-start
  520.8 8.0 collective-permute-start
  528.7 8.0 collective-permute-start
  (9 other events, 141.6 us)
Sparse Core Ops, SparseCore 0:
  39.1 420.7 all-gather.4
  573.8 412.3 all-gather.6
where the time goes:
time: 1350 us; the launch traced here: 1340 us
  waiting for transfers between devices  722 us (53%)
  other arithmetic  416 us (31%)
  local copies, waits for them, and re-layouts  69 us (5%)
  matrix products  55.5 us (4%)
  loops' own time  45.9 us (3%)
  between operations  19.1 us (1%)
    all_gather x1, waiting for transfers between devices, local(): lax.all_gather(schur[:per_device], ('row', 'panel'), axis=0, tiled=True)  412 us
    ppermute x63, waiting for transfers between devices, from_behind(): return lax.ppermute(block, axis, route)  283 us
    another operation x31, other arithmetic, local(): diag_factor = jnp.linalg.cholesky(diag_rows)  173 us
    reduce_sum x1024, other arithmetic, accumulate(): jnp.sum(jnp.exp(-(apart_east * apart_east + apart_north * apart_north) *...  148 us
    another operation x3, other arithmetic, local(): lax.linalg.triangular_solve(diag_factor, schur, left_side=False, lower=Tr...  83.7 us
    another operation x64, loops' own time, cover_tile(): total = lax.fori_loop(0, count, accumulate, start)  43 us
  transfers between devices with their start and end apart: 66, of which 64 were waited for; matrix products, arithmetic and copies ran while one was open for 13% of the time, Pallas kernels for 0%

commit v1 on v0

--- a/solution.py
+++ b/solution.py
@@ -84,7 +84,16 @@
         preferred_element_type=jnp.float32,
     )
     schur = cover - update
-    diag_rows = lax.all_gather(schur[:per_device], ("row", "panel"), axis=0, tiled=True)
+
+    def start_views_up(view, net_axis, out_dim):
+        return jnp.concatenate(
+            jax.lax.all_to_all(
+                jnp.stack([view for _ in range(jax.lax.axis_size(net_axis))]), net_axis, 0, 0
+            ),
+            axis=out_dim,
+        )
+
+    diag_rows = start_views_up(schur[:per_device], ("row", "panel"), 0)
     diag_factor = jnp.linalg.cholesky(diag_rows)
     return lax.linalg.triangular_solve(
         diag_factor, schur, left_side=False, lower=True, transpose_a=True

time: 1350 us -> 1050 us (0.78)
  waiting for transfers between devices: 722 us -> 406 us
    all_gather x1 -> x0, waiting for transfers between devices: 412 us -> none  [local(): lax.all_gather(schur[:per_device], ('row', 'panel'), axis=0, tiled=True)]
    all_to_all x0 -> x1, waiting for transfers between devices: none -> 96.2 us  [start_views_up(): jax.lax.all_to_all(jnp.stack([view for _ in range(jax.lax.axis_size(net_a...]
  transfers between devices with their start and end apart: 66 -> 66, of which waited for: 64 -> 64; matrix products, arithmetic and copies ran while one was open for 13% -> 17% of each run, Pallas kernels for 0% -> 0%
where the time goes in v1:
time: 1050 us; the launch traced here: 1040 us
  other arithmetic  416 us (40%)
  waiting for transfers between devices  406 us (39%)
  local copies, waits for them, and re-layouts  71.2 us (7%)
  matrix products  55.5 us (5%)
  loops' own time  45.9 us (4%)
  starting transfers between devices  23.9 us (2%)
  between operations  19.3 us (2%)
    ppermute x63, waiting for transfers between devices, from_behind(): return lax.ppermute(block, axis, route)  283 us
    another operation x31, other arithmetic, local(): diag_factor = jnp.linalg.cholesky(diag_rows)  173 us
    reduce_sum x1024, other arithmetic, accumulate(): jnp.sum(jnp.exp(-(apart_east * apart_east + apart_north * apart_north) *...  148 us
    all_to_all x1, waiting for transfers between devices, start_views_up(): jax.lax.all_to_all(jnp.stack([view for _ in range(jax.lax.axis_size(net_a...  96.2 us
    another operation x3, other arithmetic, local(): lax.linalg.triangular_solve(diag_factor, schur, left_side=False, lower=Tr...  83.7 us
    another operation x64, loops' own time, cover_tile(): total = lax.fori_loop(0, count, accumulate, start)  43 us
    all_to_all x1, waiting for transfers between devices, local(): lax.all_to_all(prior_factor, 'panel', split_axis=0, concat_axis=1, tiled=...  26.9 us
    another operation x14, matrix products, local(): diag_factor = jnp.linalg.cholesky(diag_rows)  23.1 us
  transfers between devices with their start and end apart: 66, of which 64 were waited for; matrix products, arithmetic and copies ran while one was open for 17% of the time, Pallas kernels for 0%

profile of v1, /device:TPU:32, one launch (start us, length us, event | category | flops | bytes accessed | tf_op | source)
XLA Modules:
  0.0 1038.0 jit_solution(3331568839337147262)
XLA Ops:
  11.4 26.9 %all-to-all-done = f32[4,256,512]{2,1,0:T(8,128)S(1)} async-done(((f32[4,256,512]{2,1,0:T(8,128)}), f32[4,256,512]{2,1,0:T(8,128)S(1)}, u32[]{:S(2)}, u32[]{:S(2)}) %all-to-all-start) | async-done | bytes 2097184 | tf_op jit(solution)/shard_map/all_to_all | solution.py:78
  39.0 497.6 %while.68 = (s32[]{:T(128)}, f32[2,16,16]{2,1,0:T(8,128)S(1)}, f32[256,1024]{0,1:T(8,128)S(1)}, f32[16,256]{1,0:T(8,128)S(1)}, f32[16,256]{1,0:T(8,128)S(1)}, /*...) while((s32[]{:T(128)}, f32[2,16,16]{2,1,0:T(8,128)S(1)}, ...), condition=%wide.region_4.5_spmd, body=%wide.region_0.4_spmd.sunk | while | flops 466965 | bytes 123403 | solution.py:71
  62.1 4.6 collective-permute-done
  70.1 4.7 collective-permute-done
  86.0 4.8 collective-permute-done
  102.1 4.6 collective-permute-done
  110.1 4.7 collective-permute-done
  126.0 4.6 collective-permute-done
  134.0 4.7 collective-permute-done
  149.9 4.6 collective-permute-done
  157.8 4.7 collective-permute-done
  173.8 4.6 collective-permute-done
  181.7 4.6 collective-permute-done
  189.7 4.7 collective-permute-done
  213.6 4.7 collective-permute-done
  221.5 4.7 collective-permute-done
  245.4 4.7 collective-permute-done
  253.4 4.6 collective-permute-done
  269.3 4.6 collective-permute-done
  277.3 4.7 collective-permute-done
  301.1 4.7 collective-permute-done
  325.0 4.7 collective-permute-done
  333.0 4.7 collective-permute-done
  356.9 4.6 collective-permute-done
  364.8 4.7 collective-permute-done
  380.7 4.6 collective-permute-done
  388.7 4.6 collective-permute-done
  396.7 4.7 collective-permute-done
  412.6 4.6 collective-permute-done
  420.6 4.7 collective-permute-done
  436.5 4.6 collective-permute-done
  444.4 4.6 collective-permute-done
  452.4 4.6 collective-permute-done
  460.4 4.6 collective-permute-done
  468.3 4.6 collective-permute-done
  476.3 4.6 collective-permute-done
  484.2 4.6 collective-permute-done
  500.2 4.6 collective-permute-done
  516.1 4.6 collective-permute-done
  524.0 4.6 collective-permute-done
  545.8 10.2 reshape.144
  556.0 16.1 %convolution_subtract_fusion = f32[256,1024]{1,0:T(8,128)S(1)} fusion(f32[256,2048]{0,1:T(8,128)S(1)} %bitcast.150, f32[1024,2048]{1,0:T(8,128)} %reshape.144, f32[256,1024]{1,0:T(8,128)S(1)} %dynamic_update_slice.13, s32[256]{0:T(256)S(1)} %iota_add_fusion, pred[256]{0:T(512)(128)(4,1)S(1)} %iota_compare_fusion.4), kind=kOutput, calls=%fused_computation.15 | convolution fusion | flops 6443761664 | bytes 12584192 | tf_op jit(solution)/shard_map/dot_general | solution.py:80
  576.1 13.2 %all-to-all-start.1 = ((f32[256,4,1024]{2,1,0:T(4,128)}), f32[256,4,1024]{2,1,0:T(4,128)}, u32[]{:S(2)}, u32[]{:S(2)}) async-start(f32[256,4,1024]{2,1,0:T(4,128)} %stack.14), calls=%async_computation.1 | async-start | bytes 8388608 | tf_op jit(solution)/shard_map/all_to_all | solution.py:90
  589.3 96.2 %all-to-all-done.1 = f32[256,4,1024]{2,1,0:T(4,128)} async-done(((f32[256,4,1024]{2,1,0:T(4,128)}), f32[256,4,1024]{2,1,0:T(4,128)}, u32[]{:S(2)}, u32[]{:S(2)}) %all-to-all-start.1) | async-done | bytes 4194336 | tf_op jit(solution)/shard_map/all_to_all | solution.py:90
  685.5 5.3 reshape.119
  690.7 5.5 copy.69
  702.6 11.7 %cholesky.223 = f32[128,128]{1,0:T(8,128)S(1)} custom-call(f32[128,128]{1,0:T(8,128)S(1)} %cholesky.580), custom_call_target="Cholesky" | custom-call | tf_op jit(solution)/shard_map/jit(cholesky)/cholesky | solution.py:97
  716.9 9.8 custom-call.62
  730.6 11.9 %cholesky.244 = f32[128,128]{1,0:T(8,128)S(1)} custom-call(f32[128,128]{1,0:T(8,128)S(1)} %cholesky.584), custom_call_target="Cholesky" | custom-call | tf_op jit(solution)/shard_map/jit(cholesky)/cholesky | solution.py:97
  743.2 9.8 custom-call.63
  756.3 11.7 %cholesky.468 = f32[128,128]{1,0:T(8,128)S(1)} custom-call(f32[128,128]{1,0:T(8,128)S(1)} %cholesky.589), custom_call_target="Cholesky" | custom-call | tf_op jit(solution)/shard_map/jit(cholesky)/cholesky | solution.py:97
  768.7 9.8 custom-call.64
  782.0 12.1 %cholesky.487 = f32[128,128]{1,0:T(8,128)S(1)} custom-call(f32[128,128]{1,0:T(8,128)S(1)} %cholesky.594), custom_call_target="Cholesky" | custom-call | tf_op jit(solution)/shard_map/jit(cholesky)/cholesky | solution.py:97
  794.7 9.8 custom-call.65
  808.0 11.7 %cholesky.506 = f32[128,128]{1,0:T(8,128)S(1)} custom-call(f32[128,128]{1,0:T(8,128)S(1)} %cholesky.599), custom_call_target="Cholesky" | custom-call | tf_op jit(solution)/shard_map/jit(cholesky)/cholesky | solution.py:97
  820.4 10.0 custom-call.66
  833.7 11.7 %cholesky.526 = f32[128,128]{1,0:T(8,128)S(1)} custom-call(f32[128,128]{1,0:T(8,128)S(1)} %cholesky.604), custom_call_target="Cholesky" | custom-call | tf_op jit(solution)/shard_map/jit(cholesky)/cholesky | solution.py:97
  846.0 9.8 custom-call.67
  858.8 11.7 %cholesky.546 = f32[128,128]{1,0:T(8,128)S(1)} custom-call(f32[128,128]{1,0:T(8,128)S(1)} %cholesky.609), custom_call_target="Cholesky" | custom-call | tf_op jit(solution)/shard_map/jit(cholesky)/cholesky | solution.py:97
  871.2 9.8 custom-call.68
  883.6 11.7 %cholesky.564 = f32[128,128]{1,0:T(8,128)S(1)} custom-call(f32[128,128]{1,0:T(8,128)S(1)} %convolution_subtract_fusion.14), custom_call_target="Cholesky" | custom-call | tf_op jit(solution)/shard_map/jit(cholesky)/cholesky | solution.py:97
  906.3 4.9 select_select_fusion
  911.2 22.8 %while.69 = (s32[]{:T(128)}, f32[1024,1024]{1,0:T(8,128)}, s32[8,2]{0,1:T(2,128)S(1)}, f32[8,128,128]{2,1,0:T(8,128)S(1)}, s32[]{:T(128)}) while((s32[]{:T(128)}, f32[1024,1024]{1,0:T(8,128)}, s32[8,2]{0,1:T(2,128)S(1)}, f32[8,128,128]{2,1,0:T(8,128)S(1)}, s32[]{:T(128)}) %tuple.176), condition=%wide.while_cond, body=%wide.while_body.sunk | while | flops 2 | bytes 131189 | solution.py:98
  934.0 78.8 %custom-call.69 = f32[8,128,128]{1,2,0:T(8,128)S(1)} custom-call(f32[8,128,128]{2,1,0:T(8,128)S(1)} %get-tuple-element.405), custom_call_target="InvertDiagBlocksLowerTriangular" | custom-call | tf_op jit(solution)/shard_map/triangular_solve | solution.py:98
  (3597 shorter events, 583.8 us)
Async XLA Ops:
  6.5 31.8 %all-to-all-start = ((f32[4,256,512]{2,1,0:T(8,128)}), f32[4,256,512]{2,1,0:T(8,128)S(1)}, u32[]{:S(2)}, u32[]{:S(2)}) async-start(f32[4,256,512]{2,1,0:T(8,128)} %bitcast.151), calls=%async_computation | async-start | bytes 4194304 | tf_op jit(solution)/shard_map/all_to_all | solution.py:78
  11.1 534.7 %all-gather.3.cloned.1.call-start = ((), (), s32[]{:S(2)}) async-start(), calls=%async_computation.2 | async-start | bytes 8421376 | tf_op jit(solution)/shard_map/all_gather | solution.py:79
  50.9 8.0 collective-permute-start
  58.8 8.0 collective-permute-start
  66.8 8.0 collective-permute-start
  74.8 7.9 collective-permute-start
  82.7 8.2 collective-permute-start
  90.9 7.9 collective-permute-start
  98.8 8.0 collective-permute-start
  106.8 8.0 collective-permute-start
  114.8 7.9 collective-permute-start
  122.7 8.0 collective-permute-start
  130.6 8.0 collective-permute-start
  138.6 7.9 collective-permute-start
  146.6 8.0 collective-permute-start
  154.5 8.0 collective-permute-start
  162.5 7.9 collective-permute-start
  170.4 8.0 collective-permute-start
  178.4 8.0 collective-permute-start
  186.4 8.0 collective-permute-start
  194.4 7.9 collective-permute-start
  202.3 7.9 collective-permute-start
  210.3 8.0 collective-permute-start
  218.2 8.0 collective-permute-start
  226.3 7.9 collective-permute-start
  234.2 7.9 collective-permute-start
  242.1 8.0 collective-permute-start
  250.1 8.0 collective-permute-start
  258.1 7.9 collective-permute-start
  266.0 8.0 collective-permute-start
  273.9 8.0 collective-permute-start
  282.0 7.9 collective-permute-start
  289.9 7.9 collective-permute-start
  297.8 8.0 collective-permute-start
  305.8 7.9 collective-permute-start
  313.8 7.9 collective-permute-start
  321.7 8.0 collective-permute-start
  329.7 8.0 collective-permute-start
  337.7 7.9 collective-permute-start
  345.6 7.9 collective-permute-start
  353.6 8.0 collective-permute-start
  361.5 8.0 collective-permute-start
  369.5 7.9 collective-permute-start
  377.4 8.0 collective-permute-start
  385.4 8.0 collective-permute-start
  393.4 8.0 collective-permute-start
  401.4 7.9 collective-permute-start
  409.3 8.0 collective-permute-start
  417.2 8.0 collective-permute-start
  425.2 7.9 collective-permute-start
  433.2 8.0 collective-permute-start
  441.1 8.0 collective-permute-start
  449.1 8.0 collective-permute-start
  457.0 8.0 collective-permute-start
  465.0 8.0 collective-permute-start
  473.0 8.0 collective-permute-start
  480.9 8.0 collective-permute-start
  488.9 8.0 collective-permute-start
  496.9 8.0 collective-permute-start
  504.8 8.0 collective-permute-start
  512.8 8.0 collective-permute-start
  520.7 8.0 collective-permute-start
  528.7 8.0 collective-permute-start
  576.1 109.4 %all-to-all-start.1 = ((f32[256,4,1024]{2,1,0:T(4,128)}), f32[256,4,1024]{2,1,0:T(4,128)}, u32[]{:S(2)}, u32[]{:S(2)}) async-start(f32[256,4,1024]{2,1,0:T(4,128)} %stack.14), calls=%async_computation.1 | async-start | bytes 8388608 | tf_op jit(solution)/shard_map/all_to_all | solution.py:90
  (9 other events, 141.6 us)
Sparse Core Ops, SparseCore 0:
  39.1 420.9 all-gather.2
